TPU v7x, 32 devices: a whole 2x2x4 slice. The times are simulated.
32 devices in a mesh: fsdp: 4 (over z), ctx: 2 (over x), tp: 4 (over y, core).
Axes of the slice: x: 2, y: 2, z: 4, core: 2. Of those that a mesh axis runs over, the one named last changes fastest.
Arguments:
- tokens: bfloat16 [8, 1024, 1024], P('fsdp', ('ctx', 'tp')), may hold values from -6 to 6
- key_valid: int32 [8, 1024], P('fsdp'), may hold values from 0 to 1, as said below
- first_gain: bfloat16 [2, 1024], P(None, 'fsdp'), may hold values from 0.25 to 1.75
- first_shift: bfloat16 [2, 1024], P(None, 'fsdp'), may hold values from -1.75 to 1.75
- joint_weight: bfloat16 [2, 1024, 3, 1024], P(None, 'fsdp', None, 'tp'), may hold values from -0.1875 to 0.1875
- query_bias: bfloat16 [2, 16, 64], P(None, 'tp', 'fsdp'), may hold values from -3 to 3
- value_bias: bfloat16 [2, 16, 64], P(None, 'tp', 'fsdp'), may hold values from -0.625 to 0.625
- out_weight: bfloat16 [2, 1024, 1024], P(None, 'tp', 'fsdp'), may hold values from -0.75 to 0.75
- out_bias: bfloat16 [2, 1024], P(None, 'fsdp'), may hold values from -1.75 to 1.75
- second_gain: bfloat16 [2, 1024], P(None, 'fsdp'), may hold values from 0.25 to 1.75
- second_shift: bfloat16 [2, 1024], P(None, 'fsdp'), may hold values from -1.75 to 1.75
- expand_weight: bfloat16 [2, 1024, 4096], P(None, 'fsdp', 'tp'), may hold values from -0.1875 to 0.1875
- expand_bias: bfloat16 [2, 64, 64], P(None, 'tp', 'fsdp'), may hold values from -3 to 3
- reduce_weight: bfloat16 [2, 4096, 1024], P(None, 'tp', 'fsdp'), may hold values from -0.09375 to 0.09375
- reduce_bias: bfloat16 [2, 1024], P(None, 'fsdp'), may hold values from -1.75 to 1.75
- cotangent: bfloat16 [8, 1024, 1024], P('fsdp', ('ctx', 'tp')), may hold values from -6 to 6
Outputs:
- output: bfloat16 [8, 1024, 1024], P('fsdp', ('ctx', 'tp'))
- input_grad: bfloat16 [8, 1024, 1024], P('fsdp', ('ctx', 'tp'))
- grad_first_gain: float32 [2, 1024], P(None, 'fsdp')
- grad_first_shift: float32 [2, 1024], P(None, 'fsdp')
- grad_joint_weight: float32 [2, 1024, 3, 1024], P(None, 'fsdp', None, 'tp')
- grad_query_bias: float32 [2, 16, 64], P(None, 'tp', 'fsdp')
- grad_value_bias: float32 [2, 16, 64], P(None, 'tp', 'fsdp')
- grad_out_weight: float32 [2, 1024, 1024], P(None, 'tp', 'fsdp')
- grad_out_bias: float32 [2, 1024], P(None, 'fsdp')
- grad_second_gain: float32 [2, 1024], P(None, 'fsdp')
- grad_second_shift: float32 [2, 1024], P(None, 'fsdp')
- grad_expand_weight: float32 [2, 1024, 4096], P(None, 'fsdp', 'tp')
- grad_expand_bias: float32 [2, 64, 64], P(None, 'tp', 'fsdp')
- grad_reduce_weight: float32 [2, 4096, 1024], P(None, 'tp', 'fsdp')
- grad_reduce_bias: float32 [2, 1024], P(None, 'fsdp')
Inputs may be any that keep to these rules, and one draw needn't show every extreme that they name: `key_valid`: in each clip the ones form a prefix of 128 tokens or more; clip 0 has ones throughout.
All inputs are finite; a program needn't handle non-finite values.
Results may differ from a plain program's by a relative error of at most 0.02.
Values may be sent and summed in bfloat16 or wider, within the bound.
A program may use at most 256 MiB of HBM per device.

v0:
```python
import jax
import jax.numpy as jnp
from jax import lax
from jax.sharding import PartitionSpec as P

HD = 64
LAYERS = 2
MB = 2
epsilon = 1e-06
masked_score = -10000.0


def norm_rows(rows, gain, shift):
    middle = jnp.mean(rows, axis=-1, keepdims=True)
    centred = rows - middle
    spread = jnp.mean(centred * centred, axis=-1, keepdims=True)
    return centred * lax.rsqrt(spread + epsilon) * gain + shift


def exact_gelu(values):
    return jax.nn.gelu(values, approximate=False)


def dense(left, right):
    return jnp.dot(left, right, preferred_element_type=jnp.float32)


def dense_left(left, right):
    return lax.dot_general(
        left, right, (((0,), (0,)), ((), ())), preferred_element_type=jnp.float32
    )


def dense_right(left, right):
    return lax.dot_general(
        left, right, (((1,), (1,)), ((), ())), preferred_element_type=jnp.float32
    )


def head_major(rows):
    return rows.reshape(rows.shape[0], -1, HD).transpose(1, 0, 2)


def row_major(heads):
    return heads.transpose(1, 0, 2).reshape(heads.shape[1], -1)


def spread_rows(rows):
    return lax.all_gather(rows, "tp", axis=0, tiled=True)


def gather_grad(rows):
    return lax.all_gather(rows, "tp", axis=0, tiled=True)


def combine_rows(partial_value):
    return lax.psum_scatter(
        partial_value.astype(jnp.bfloat16), "tp", scatter_dimension=0, tiled=True
    ).astype(jnp.float32)


def combine_grads(partial_value):
    return lax.psum_scatter(
        partial_value.astype(jnp.bfloat16), "tp", scatter_dimension=0, tiled=True
    ).astype(jnp.float32)


def fetch(params, layer_id):
    (
        first_gain,
        first_shift,
        joint_weight,
        query_bias,
        value_bias,
        out_weight,
        out_bias,
        second_gain,
        second_shift,
        expand_weight,
        expand_bias,
        reduce_weight,
        reduce_bias,
    ) = params
    return (
        lax.all_gather(first_gain[layer_id], "fsdp", axis=0, tiled=True),
        lax.all_gather(first_shift[layer_id], "fsdp", axis=0, tiled=True),
        lax.all_gather(joint_weight[layer_id], "fsdp", axis=0, tiled=True),
        lax.all_gather(query_bias[layer_id], "fsdp", axis=1, tiled=True),
        lax.all_gather(value_bias[layer_id], "fsdp", axis=1, tiled=True),
        lax.all_gather(out_weight[layer_id], "fsdp", axis=1, tiled=True),
        lax.all_gather(out_bias[layer_id], "fsdp", axis=0, tiled=True),
        lax.all_gather(second_gain[layer_id], "fsdp", axis=0, tiled=True),
        lax.all_gather(second_shift[layer_id], "fsdp", axis=0, tiled=True),
        lax.all_gather(expand_weight[layer_id], "fsdp", axis=0, tiled=True),
        lax.all_gather(expand_bias[layer_id], "fsdp", axis=1, tiled=True),
        lax.all_gather(reduce_weight[layer_id], "fsdp", axis=1, tiled=True),
        lax.all_gather(reduce_bias[layer_id], "fsdp", axis=0, tiled=True),
    )


def attention_scores(query_heads, key_heads, key_bias):
    raw_scores = jnp.einsum(
        "hqd,hkd->hqk", query_heads, key_heads, preferred_element_type=jnp.float32
    )
    return raw_scores * HD ** (-0.5) + key_bias


def forward_layer(residual, layer_weights, key_bias):
    (
        gain_attn,
        shift_attn,
        joint_mat,
        query_add,
        value_add,
        out_mat,
        out_add,
        gain_mlp,
        shift_mlp,
        expand_mat,
        expand_add,
        reduce_mat,
        reduce_add,
    ) = layer_weights
    normed = norm_rows(residual, gain_attn.astype(jnp.float32), shift_attn.astype(jnp.float32))
    first_in = spread_rows(normed.astype(jnp.bfloat16))
    joint = jnp.einsum("nd,dce->nce", first_in, joint_mat, preferred_element_type=jnp.float32)
    queries = (joint[:, 0] + query_add.reshape(-1).astype(jnp.float32)).astype(jnp.bfloat16)
    keys_local = joint[:, 1].astype(jnp.bfloat16)
    values_local = (joint[:, 2] + value_add.reshape(-1).astype(jnp.float32)).astype(jnp.bfloat16)
    keys_all, values_all = (
        lax.all_gather(keys_local, "ctx", axis=0, tiled=True),
        lax.all_gather(values_local, "ctx", axis=0, tiled=True),
    )
    query_heads = head_major(queries)
    key_heads = head_major(keys_all)
    value_heads = head_major(values_all)
    scores = attention_scores(query_heads, key_heads, key_bias)
    row_top = jnp.max(scores, axis=-1, keepdims=True)
    exponent = jnp.exp(scores - row_top)
    row_total = jnp.sum(exponent, axis=-1, keepdims=True)
    probs_low = (exponent / row_total).astype(jnp.bfloat16)
    log_total = row_top + jnp.log(row_total)
    mixed_heads = jnp.einsum(
        "hqk,hkd->hqd", probs_low, value_heads, preferred_element_type=jnp.float32
    )
    mixed = row_major(mixed_heads.astype(jnp.bfloat16))
    middle = residual + (combine_rows(dense(mixed, out_mat)) + out_add.astype(jnp.float32))
    normed_mlp = norm_rows(middle, gain_mlp.astype(jnp.float32), shift_mlp.astype(jnp.float32))
    second_in = spread_rows(normed_mlp.astype(jnp.bfloat16))
    before = dense(second_in, expand_mat) + expand_add.reshape(-1).astype(jnp.float32)
    active = exact_gelu(before).astype(jnp.bfloat16)
    result = middle + (combine_rows(dense(active, reduce_mat)) + reduce_add.astype(jnp.float32))
    stored = (
        residual,
        first_in,
        query_heads,
        key_heads,
        value_heads,
        log_total,
        mixed,
        middle,
        second_in,
        before,
        active,
    )
    return (result, stored)


def backward_layer(carry, stored, layer_weights, key_bias):
    (
        gain_attn,
        shift_attn,
        joint_mat,
        query_add,
        value_add,
        out_mat,
        out_add,
        gain_mlp,
        shift_mlp,
        expand_mat,
        expand_add,
        reduce_mat,
        reduce_add,
    ) = layer_weights
    (
        residual,
        first_in,
        query_heads,
        key_heads,
        value_heads,
        log_total,
        mixed,
        middle,
        second_in,
        before,
        active,
    ) = stored
    low_mlp = carry.astype(jnp.bfloat16)
    mlp_rows = gather_grad(low_mlp)
    d_reduce_mat = dense_left(active, mlp_rows)
    d_reduce_add = jnp.sum(low_mlp.astype(jnp.float32), axis=0)
    d_active = dense_right(mlp_rows, reduce_mat)
    gelu_value, gelu_back = jax.vjp(exact_gelu, before)
    d_before = gelu_back(d_active)[0].astype(jnp.bfloat16)
    d_expand_add = jnp.sum(d_before.astype(jnp.float32), axis=0).reshape(expand_add.shape)
    d_expand_mat = dense_left(second_in, d_before)
    d_second = combine_grads(dense_right(d_before, expand_mat))
    norm_value, norm_back = jax.vjp(
        norm_rows, middle, gain_mlp.astype(jnp.float32), shift_mlp.astype(jnp.float32)
    )
    d_middle, d_gain_mlp, d_shift_mlp = norm_back(d_second)
    carry_mid = carry + d_middle
    low_attn = carry_mid.astype(jnp.bfloat16)
    attn_rows = gather_grad(low_attn)
    d_out_mat = dense_left(mixed, attn_rows)
    d_out_add = jnp.sum(low_attn.astype(jnp.float32), axis=0)
    d_mixed = head_major(dense_right(attn_rows, out_mat).astype(jnp.bfloat16))
    scores = attention_scores(query_heads, key_heads, key_bias)
    attn_probs = jnp.exp(scores - log_total)
    d_values = jnp.einsum(
        "hqk,hqd->hkd", attn_probs.astype(jnp.bfloat16), d_mixed, preferred_element_type=jnp.float32
    )
    d_probs = jnp.einsum("hqd,hkd->hqk", d_mixed, value_heads, preferred_element_type=jnp.float32)
    d_scores = attn_probs * (d_probs - jnp.sum(attn_probs * d_probs, axis=-1, keepdims=True))
    d_raw = (d_scores * HD ** (-0.5)).astype(jnp.bfloat16)
    d_queries = jnp.einsum("hqk,hkd->hqd", d_raw, key_heads, preferred_element_type=jnp.float32)
    d_queries = row_major(d_queries.astype(jnp.bfloat16))
    d_keys = jnp.einsum("hqk,hqd->hkd", d_raw, query_heads, preferred_element_type=jnp.float32)
    d_keys = row_major(d_keys)
    d_values = row_major(d_values)
    d_keys, d_values = (
        lax.psum_scatter(
            d_keys.astype(jnp.bfloat16), "ctx", scatter_dimension=0, tiled=True
        ).astype(jnp.float32),
        lax.psum_scatter(
            d_values.astype(jnp.bfloat16), "ctx", scatter_dimension=0, tiled=True
        ).astype(jnp.float32),
    )
    d_keys = d_keys.astype(jnp.bfloat16)
    d_values = d_values.astype(jnp.bfloat16)
    d_joint = jnp.stack((d_queries, d_keys, d_values), axis=1)
    d_joint_mat = jnp.einsum("nd,nce->dce", first_in, d_joint, preferred_element_type=jnp.float32)
    d_query_add = jnp.sum(d_queries.astype(jnp.float32), axis=0).reshape(query_add.shape)
    d_value_add = jnp.sum(d_values.astype(jnp.float32), axis=0).reshape(value_add.shape)
    d_first = combine_grads(
        jnp.einsum("nce,dce->nd", d_joint, joint_mat, preferred_element_type=jnp.float32)
    )
    first_value, first_back = jax.vjp(
        norm_rows, residual, gain_attn.astype(jnp.float32), shift_attn.astype(jnp.float32)
    )
    d_residual, d_gain_attn, d_shift_attn = first_back(d_first)
    carry_in = carry_mid + d_residual
    layer_grads = (
        d_gain_attn,
        d_shift_attn,
        d_joint_mat,
        d_query_add,
        d_value_add,
        d_out_mat,
        d_out_add,
        d_gain_mlp,
        d_shift_mlp,
        d_expand_mat,
        d_expand_add,
        d_reduce_mat,
        d_reduce_add,
    )
    return (carry_in, layer_grads)


def local(
    tokens,
    key_valid,
    first_gain,
    first_shift,
    joint_weight,
    query_bias,
    value_bias,
    out_weight,
    out_bias,
    second_gain,
    second_shift,
    expand_weight,
    expand_bias,
    reduce_weight,
    reduce_bias,
    cotangent,
):
    params = (
        first_gain,
        first_shift,
        joint_weight,
        query_bias,
        value_bias,
        out_weight,
        out_bias,
        second_gain,
        second_shift,
        expand_weight,
        expand_bias,
        reduce_weight,
        reduce_bias,
    )
    fetched = tuple((fetch(params, layer_id) for layer_id in range(LAYERS)))
    totals = [None] * LAYERS
    outputs = []
    row_grads = []
    for batch_id in range(MB):
        key_bias = jnp.where(key_valid[batch_id] == 1, 0.0, masked_score).astype(jnp.float32)
        residual = tokens[batch_id].astype(jnp.float32)
        stores = []
        for layer_id in range(LAYERS):
            residual, stored = forward_layer(residual, fetched[layer_id], key_bias)
            stores.append(stored)
        outputs.append(residual.astype(jnp.bfloat16))
        carry = cotangent[batch_id].astype(jnp.float32)
        for layer_id in reversed(range(LAYERS)):
            carry, layer_grads = backward_layer(
                carry, stores[layer_id], fetched[layer_id], key_bias
            )
            if totals[layer_id] is None:
                totals[layer_id] = layer_grads
            else:
                totals[layer_id] = tuple(
                    (old + new for old, new in zip(totals[layer_id], layer_grads))
                )
        row_grads.append(carry.astype(jnp.bfloat16))
    stacked = [
        jnp.stack([totals[layer_id][index] for layer_id in range(LAYERS)]) for index in range(13)
    ]
    shards = (
        lax.psum_scatter(
            stacked[0].astype(jnp.bfloat16), "fsdp", scatter_dimension=1, tiled=True
        ).astype(jnp.float32),
        lax.psum_scatter(
            stacked[1].astype(jnp.bfloat16), "fsdp", scatter_dimension=1, tiled=True
        ).astype(jnp.float32),
        lax.psum_scatter(
            stacked[2].astype(jnp.bfloat16), "fsdp", scatter_dimension=1, tiled=True
        ).astype(jnp.float32),
        lax.psum_scatter(
            stacked[3].astype(jnp.bfloat16), "fsdp", scatter_dimension=2, tiled=True
        ).astype(jnp.float32),
        lax.psum_scatter(
            stacked[4].astype(jnp.bfloat16), "fsdp", scatter_dimension=2, tiled=True
        ).astype(jnp.float32),
        lax.psum_scatter(
            stacked[5].astype(jnp.bfloat16), "fsdp", scatter_dimension=2, tiled=True
        ).astype(jnp.float32),
        lax.psum_scatter(
            stacked[6].astype(jnp.bfloat16), "fsdp", scatter_dimension=1, tiled=True
        ).astype(jnp.float32),
        lax.psum_scatter(
            stacked[7].astype(jnp.bfloat16), "fsdp", scatter_dimension=1, tiled=True
        ).astype(jnp.float32),
        lax.psum_scatter(
            stacked[8].astype(jnp.bfloat16), "fsdp", scatter_dimension=1, tiled=True
        ).astype(jnp.float32),
        lax.psum_scatter(
            stacked[9].astype(jnp.bfloat16), "fsdp", scatter_dimension=1, tiled=True
        ).astype(jnp.float32),
        lax.psum_scatter(
            stacked[10].astype(jnp.bfloat16), "fsdp", scatter_dimension=2, tiled=True
        ).astype(jnp.float32),
        lax.psum_scatter(
            stacked[11].astype(jnp.bfloat16), "fsdp", scatter_dimension=2, tiled=True
        ).astype(jnp.float32),
        lax.psum_scatter(
            stacked[12].astype(jnp.bfloat16), "fsdp", scatter_dimension=1, tiled=True
        ).astype(jnp.float32),
    )
    split_sums = (
        lax.psum(shards[2].astype(jnp.bfloat16), "ctx").astype(jnp.float32),
        lax.psum(shards[3].astype(jnp.bfloat16), "ctx").astype(jnp.float32),
        lax.psum(shards[4].astype(jnp.bfloat16), "ctx").astype(jnp.float32),
        lax.psum(shards[5].astype(jnp.bfloat16), "ctx").astype(jnp.float32),
        lax.psum(shards[9].astype(jnp.bfloat16), "ctx").astype(jnp.float32),
        lax.psum(shards[10].astype(jnp.bfloat16), "ctx").astype(jnp.float32),
        lax.psum(shards[11].astype(jnp.bfloat16), "ctx").astype(jnp.float32),
    )
    vector_part = lax.psum(
        (shards[0], shards[1], shards[6], shards[7], shards[8], shards[12]), ("ctx", "tp")
    )
    return (
        jnp.stack(outputs),
        jnp.stack(row_grads),
        vector_part[0],
        vector_part[1],
        split_sums[0],
        split_sums[1],
        split_sums[2],
        split_sums[3],
        vector_part[2],
        vector_part[3],
        vector_part[4],
        split_sums[4],
        split_sums[5],
        split_sums[6],
        vector_part[5],
    )


def solution(mesh):
    placed = (
        P("fsdp", ("ctx", "tp"), None),
        P("fsdp", None),
        P(None, "fsdp"),
        P(None, "fsdp"),
        P(None, "fsdp", None, "tp"),
        P(None, "tp", "fsdp"),
        P(None, "tp", "fsdp"),
        P(None, "tp", "fsdp"),
        P(None, "fsdp"),
        P(None, "fsdp"),
        P(None, "fsdp"),
        P(None, "fsdp", "tp"),
        P(None, "tp", "fsdp"),
        P(None, "tp", "fsdp"),
        P(None, "fsdp"),
        P("fsdp", ("ctx", "tp"), None),
    )
    return jax.shard_map(
        local,
        mesh=mesh,
        in_specs=placed,
        out_specs=(
            P("fsdp", ("ctx", "tp"), None),
            P("fsdp", ("ctx", "tp"), None),
            P(None, "fsdp"),
            P(None, "fsdp"),
            P(None, "fsdp", None, "tp"),
            P(None, "tp", "fsdp"),
            P(None, "tp", "fsdp"),
            P(None, "tp", "fsdp"),
            P(None, "fsdp"),
            P(None, "fsdp"),
            P(None, "fsdp"),
            P(None, "fsdp", "tp"),
            P(None, "tp", "fsdp"),
            P(None, "tp", "fsdp"),
            P(None, "fsdp"),
        ),
        check_vma=False,
    )
```

profile of v0, /device:TPU:0, one launch (start us, length us, event | category | flops | bytes accessed | tf_op | source)
XLA Modules:
  0.0 1841.4 jit_solution(5257562722936392963)
XLA Ops:
  61.3 19.5 %all-gather.6 = bf16[1,256,1024]{2,1,0:T(8,128)(2,1)S(1)} all-gather(bf16[1,256,256]{2,1,0:T(8,128)(2,1)S(1)} %get-tuple-element.130), channel_id=8, replica_groups=mesh['fsdp'=4,'ctx'=2,'tp'=4] {'fsdp'}, dimensions={2}, use_global_device_ids=true | all-gather | bytes 655360 | tf_op jit(solution)/shard_map/all_gather | solution.py:90
  132.0 15.0 reduce-scatter.56.cloned.1.call-done
  149.2 16.8 all-gather.63.cloned.1.call-done
  227.0 13.6 all-gather.11
  240.8 27.9 %all-gather.85.cloned.1.call-done = bf16[1,1024,1024]{2,1,0:T(8,128)(2,1)} async-done(((bf16[1,256,1024]{2,1,0:T(8,128)(2,1)}), bf16[1,1024,1024]{2,1,0:T(8,128)(2,1)}) %all-gather.85.cloned.1.call-update) | async-done | bytes 2097168 | tf_op jit(solution)/shard_map/all_gather | solution.py:94
  268.7 17.6 all-gather.65.cloned.1.call-done
  290.8 14.4 all-gather.57.cloned.1.call-done
  305.2 13.4 multiply_convert_fusion.7
  318.6 35.0 %all-gather.87.cloned.1.call-done = bf16[1,1024,1024]{2,1,0:T(8,128)(2,1)} async-done(((bf16[1,1024,256]{2,1,0:T(8,128)(2,1)}), bf16[1,1024,1024]{2,1,0:T(8,128)(2,1)}) %all-gather.87.cloned.1.call-update) | async-done | bytes 2097168 | tf_op jit(solution)/shard_map/all_gather | solution.py:96
  388.2 20.1 %reduce-scatter.66.cloned.1.call-done = bf16[128,1024]{1,0:T(8,128)(2,1)} async-done(((bf16[512,1024]{1,0:T(8,128)(2,1)}), bf16[128,1024]{1,0:T(8,128)(2,1)}) %reduce-scatter.66.cloned.1.call-update) | async-done | bytes 262160 | tf_op jit(solution)/shard_map/reduce_scatter | solution.py:57
  425.4 18.0 all-gather.19
  443.6 17.2 all-gather.20
  583.7 13.4 all-gather.25
  597.3 27.3 %all-gather.91.cloned.1.call-done = bf16[1,1024,1024]{2,1,0:T(8,128)(2,1)} async-done(((bf16[1,256,1024]{2,1,0:T(8,128)(2,1)}), bf16[1,1024,1024]{2,1,0:T(8,128)(2,1)}) %all-gather.91.cloned.1.call-update) | async-done | bytes 2097168 | tf_op jit(solution)/shard_map/all_gather | solution.py:94
  624.6 17.1 all-gather.69.cloned.1.call-done
  646.2 14.3 all-gather.61.cloned.1.call-done
  660.6 13.8 multiply_convert_fusion.6
  678.8 48.4 %all-gather.93.cloned.1.call-done = bf16[1,1024,1024]{2,1,0:T(8,128)(2,1)} async-done(((bf16[1,1024,256]{2,1,0:T(8,128)(2,1)}), bf16[1,1024,1024]{2,1,0:T(8,128)(2,1)}) %all-gather.93.cloned.1.call-update) | async-done | bytes 2097168 | tf_op jit(solution)/shard_map/all_gather | solution.py:96
  771.9 26.8 %reduce-scatter.72.cloned.1.call-done = bf16[128,1024]{1,0:T(8,128)(2,1)} async-done(((bf16[512,1024]{1,0:T(8,128)(2,1)}), bf16[128,1024]{1,0:T(8,128)(2,1)}) %reduce-scatter.72.cloned.1.call-update) | async-done | bytes 262160 | tf_op jit(solution)/shard_map/reduce_scatter | solution.py:63
  800.1 26.0 %reduce-scatter.62.cloned.1.call-done = bf16[128,1024]{1,0:T(8,128)(2,1)} async-done(((bf16[512,1024]{1,0:T(8,128)(2,1)}), bf16[128,1024]{1,0:T(8,128)(2,1)}) %reduce-scatter.62.cloned.1.call-update) | async-done | bytes 262160 | tf_op jit(solution)/shard_map/reduce_scatter | solution.py:57
  826.1 27.5 %reduce-scatter.70.cloned.1.call-done = bf16[128,1024]{1,0:T(8,128)(2,1)} async-done(((bf16[512,1024]{1,0:T(8,128)(2,1)}), bf16[128,1024]{1,0:T(8,128)(2,1)}) %reduce-scatter.70.cloned.1.call-update) | async-done | bytes 262160 | tf_op jit(solution)/shard_map/reduce_scatter | solution.py:57
  858.1 16.1 all-gather.77.cloned.1.call-done
  881.5 23.0 %fusion.221 = bf16[4,1024,64]{1,2,0:T(8,128)(2,1)} fusion(f32[4,512,1024]{2,1,0:T(8,128)} %fusion.467, f32[4,512,1024]{2,1,0:T(8,128)} %copy-done.4, f32[4,512]{1,0:T(4,128)S(1)} %log_add_fusion.1, f32[1024]{0:T(1024)S(1)} %bitcast.661, f32[512,4,64]{0,2,1:T(8,128)S(1)} %bitcast.579, f32[4,64]{1,0:T(4,128)S(1)} %copy.126), kind=kOutput, calls=%fused_computation.234 | convolution fusion | flops 292031488 | bytes 17839104 | tf_op jit(solution)/shard_map/hqk,hqd->hkd/dot_general | solution.py:228
  921.5 22.2 %fusion.227 = bf16[4,1024,64]{1,2,0:T(8,128)(2,1)S(1)} fusion(f32[4,512,1024]{2,1,0:T(8,128)} %fusion.465, f32[4,512,1024]{2,1,0:T(8,128)} %copy-done.3, f32[4,512]{1,0:T(4,128)S(1)} %log_add_fusion.3, f32[1024]{0:T(1024)S(1)} %bitcast.649, f32[512,4,64]{0,2,1:T(8,128)S(1)} %bitcast.577, f32[4,64]{1,0:T(4,128)S(1)} %copy.126), kind=kOutput, calls=%fused_computation.236 | convolution fusion | flops 292031488 | bytes 17839104 | tf_op jit(solution)/shard_map/hqk,hqd->hkd/dot_general | solution.py:228
  951.3 21.7 %convert_reduce_fusion.26 = (f32[4,64]{1,0:T(4,128)S(1)}, bf16[4,512,64]{1,2,0:T(8,128)(2,1)S(1)}) fusion(bf16[4,1024,64]{1,2,0:T(8,128)(2,1)S(1)} %bitcast.575, f32[4,512,1024]{2,1,0:T(8,128)} %fusion.467, f32[4,512,1024]{2,1,0:T(8,128)} %copy-done.4, f32[4,512]{1,0:T(4,128)S(1)} %log_add_fusion.1, f32[1024]{0:T(1024)S(1)} %bitcast.663), kind=kOutput, calls=%fused_computation.405 | convolution fusion | flops 291900160 | bytes 17576960 | tf_op jit(solution)/shard_map/hqk,hkd->hqd/dot_general | solution.py:226
  977.0 21.7 %convert_reduce_fusion.27 = (f32[4,64]{1,0:T(4,128)S(1)}, bf16[4,512,64]{1,2,0:T(8,128)(2,1)S(1)}) fusion(bf16[4,1024,64]{1,2,0:T(8,128)(2,1)S(1)} %bitcast.573, f32[4,512,1024]{2,1,0:T(8,128)} %fusion.465, f32[4,512,1024]{2,1,0:T(8,128)} %copy-done.3, f32[4,512]{1,0:T(4,128)S(1)} %log_add_fusion.3, f32[1024]{0:T(1024)S(1)} %bitcast.651), kind=kOutput, calls=%fused_computation.406 | convolution fusion | flops 291900160 | bytes 17576960 | tf_op jit(solution)/shard_map/hqk,hkd->hqd/dot_general | solution.py:226
  1004.4 27.6 %reduce-scatter.78.cloned.1.call-done = bf16[128,1024]{1,0:T(8,128)(2,1)} async-done(((bf16[512,1024]{1,0:T(8,128)(2,1)}), bf16[128,1024]{1,0:T(8,128)(2,1)}) %reduce-scatter.78.cloned.1.call-update) | async-done | bytes 262160 | tf_op jit(solution)/shard_map/reduce_scatter | solution.py:63
  1037.7 16.1 all-gather.79.cloned.1.call-done
  1081.1 18.7 %reduce-scatter.96.cloned.1.call-done = bf16[128,1024]{1,0:T(8,128)(2,1)} async-done(((bf16[512,1024]{1,0:T(8,128)(2,1)}), bf16[128,1024]{1,0:T(8,128)(2,1)}) %reduce-scatter.96.cloned.1.call-update) | async-done | bytes 262160 | tf_op jit(solution)/shard_map/reduce_scatter | solution.py:63
  1099.8 28.2 %reduce-scatter.80.cloned.1.call-done = bf16[128,1024]{1,0:T(8,128)(2,1)} async-done(((bf16[512,1024]{1,0:T(8,128)(2,1)}), bf16[128,1024]{1,0:T(8,128)(2,1)}) %reduce-scatter.80.cloned.1.call-update) | async-done | bytes 262160 | tf_op jit(solution)/shard_map/reduce_scatter | solution.py:63
  1135.7 14.4 all-gather.81.cloned.1.call-done
  1157.4 22.8 %fusion.218 = bf16[4,1024,64]{1,2,0:T(8,128)(2,1)} fusion(f32[4,512,1024]{2,1,0:T(8,128)} %fusion.468, f32[4,512,1024]{2,1,0:T(8,128)} %copy-done.2, f32[4,512]{1,0:T(4,128)S(1)} %log_add_fusion, f32[1024]{0:T(1024)S(1)} %bitcast.664, f32[512,4,64]{0,2,1:T(8,128)S(1)} %bitcast.569, f32[4,64]{1,0:T(4,128)S(1)} %copy-done.104), kind=kOutput, calls=%fused_computation.233 | convolution fusion | flops 292031488 | bytes 17839104 | tf_op jit(solution)/shard_map/hqk,hqd->hkd/dot_general | solution.py:228
  1196.9 22.0 %fusion.224 = bf16[4,1024,64]{1,2,0:T(8,128)(2,1)S(1)} fusion(f32[4,512,1024]{2,1,0:T(8,128)} %fusion.466, f32[4,512,1024]{2,1,0:T(8,128)} %copy-done.1, f32[4,512]{1,0:T(4,128)S(1)} %log_add_fusion.2, f32[1024]{0:T(1024)S(1)} %bitcast.652, f32[512,4,64]{0,2,1:T(8,128)S(1)} %bitcast.563, f32[4,64]{1,0:T(4,128)S(1)} %copy-done.104), kind=kOutput, calls=%fused_computation.235 | convolution fusion | flops 292031488 | bytes 17839104 | tf_op jit(solution)/shard_map/hqk,hqd->hkd/dot_general | solution.py:228
  1226.5 22.1 %convert_reduce_fusion.28 = (f32[4,64]{1,0:T(4,128)}, bf16[4,512,64]{1,2,0:T(8,128)(2,1)S(1)}) fusion(bf16[4,1024,64]{1,2,0:T(8,128)(2,1)S(1)} %bitcast.567, f32[4,512,1024]{2,1,0:T(8,128)} %fusion.468, f32[4,512,1024]{2,1,0:T(8,128)} %copy-done.2, f32[4,512]{1,0:T(4,128)S(1)} %log_add_fusion, f32[1024]{0:T(1024)S(1)} %bitcast.666), kind=kOutput, calls=%fused_computation.407 | convolution fusion | flops 291900160 | bytes 17576960 | tf_op jit(solution)/shard_map/hqk,hkd->hqd/dot_general | solution.py:226
  1252.5 22.1 %convert_reduce_fusion.29 = (f32[4,64]{1,0:T(4,128)}, bf16[4,512,64]{1,2,0:T(8,128)(2,1)S(1)}) fusion(bf16[4,1024,64]{1,2,0:T(8,128)(2,1)S(1)} %bitcast.561, f32[4,512,1024]{2,1,0:T(8,128)} %fusion.466, f32[4,512,1024]{2,1,0:T(8,128)} %copy-done.1, f32[4,512]{1,0:T(4,128)S(1)} %log_add_fusion.2, f32[1024]{0:T(1024)S(1)} %bitcast.654), kind=kOutput, calls=%fused_computation.408 | convolution fusion | flops 291900160 | bytes 17576960 | tf_op jit(solution)/shard_map/hqk,hkd->hqd/dot_general | solution.py:226
  1337.6 77.7 %reduce-scatter.110.cloned.1.call-done = bf16[2,1024,256]{2,1,0:T(8,128)(2,1)} async-done(((bf16[2,1024,1024]{2,1,0:T(8,128)(2,1)}), bf16[2,1024,256]{2,1,0:T(8,128)(2,1)}) %reduce-scatter.110.cloned.1.call-update) | async-done | bytes 1048592 | tf_op jit(solution)/shard_map/reduce_scatter | solution.py:365
  1415.3 79.5 %reduce-scatter.108.cloned.1.call-done = bf16[2,256,1024]{2,1,0:T(8,128)(2,1)} async-done(((bf16[2,1024,1024]{2,1,0:T(8,128)(2,1)}), bf16[2,256,1024]{2,1,0:T(8,128)(2,1)}) %reduce-scatter.108.cloned.1.call-update) | async-done | bytes 1048592 | tf_op jit(solution)/shard_map/reduce_scatter | solution.py:359
  1494.7 63.2 %reduce-scatter.104.cloned.1.call-done = bf16[2,256,3,256]{3,1,2,0:T(8,128)(2,1)} async-done(((bf16[2,1024,3,256]{3,1,2,0:T(8,128)(2,1)}), bf16[2,256,3,256]{3,1,2,0:T(8,128)(2,1)}) %reduce-scatter.104.cloned.1.call-update) | async-done | bytes 786448 | tf_op jit(solution)/shard_map/reduce_scatter | solution.py:338
  1559.9 19.9 %reduce-scatter.128.cloned.1.call-done = bf16[256,2]{1,0:T(8,128)(2,1)} async-done(((bf16[1024,2]{1,0:T(8,128)(2,1)}), bf16[256,2]{1,0:T(8,128)(2,1)}) %reduce-scatter.128.cloned.1.call-update) | async-done | bytes 1040
  1580.7 18.6 %reduce-scatter.126.cloned.1.call-done = bf16[16,32]{1,0:T(8,128)(2,1)} async-done(((bf16[64,32]{1,0:T(8,128)(2,1)}), bf16[16,32]{1,0:T(8,128)(2,1)}) %reduce-scatter.126.cloned.1.call-update) | async-done | bytes 1040
  1600.1 19.1 %reduce-scatter.124.cloned.1.call-done = bf16[256,2]{1,0:T(8,128)(2,1)} async-done(((bf16[1024,2]{1,0:T(8,128)(2,1)}), bf16[256,2]{1,0:T(8,128)(2,1)}) %reduce-scatter.124.cloned.1.call-update) | async-done | bytes 1040
  1620.1 19.4 %reduce-scatter.122.cloned.1.call-done = bf16[256,2]{1,0:T(8,128)(2,1)} async-done(((bf16[1024,2]{1,0:T(8,128)(2,1)}), bf16[256,2]{1,0:T(8,128)(2,1)}) %reduce-scatter.122.cloned.1.call-update) | async-done | bytes 1040
  1640.4 19.2 %reduce-scatter.120.cloned.1.call-done = bf16[256,2]{1,0:T(8,128)(2,1)} async-done(((bf16[1024,2]{1,0:T(8,128)(2,1)}), bf16[256,2]{1,0:T(8,128)(2,1)}) %reduce-scatter.120.cloned.1.call-update) | async-done | bytes 1040
  1660.6 19.1 %reduce-scatter.116.cloned.1.call-done = bf16[16,8]{1,0:T(8,128)(2,1)} async-done(((bf16[64,8]{1,0:T(8,128)(2,1)}), bf16[16,8]{1,0:T(8,128)(2,1)}) %reduce-scatter.116.cloned.1.call-update) | async-done | bytes 272
  1680.6 18.5 %reduce-scatter.118.cloned.1.call-done = bf16[16,8]{1,0:T(8,128)(2,1)} async-done(((bf16[64,8]{1,0:T(8,128)(2,1)}), bf16[16,8]{1,0:T(8,128)(2,1)}) %reduce-scatter.118.cloned.1.call-update) | async-done | bytes 272
  1720.6 19.7 %reduce-scatter.112.cloned.1.call-done = bf16[256,2]{1,0:T(8,128)(2,1)} async-done(((bf16[1024,2]{1,0:T(8,128)(2,1)}), bf16[256,2]{1,0:T(8,128)(2,1)}) %reduce-scatter.112.cloned.1.call-update) | async-done | bytes 1040
  1741.2 22.8 %all-reduce = (f32[2,256]{1,0:T(2,128)}, f32[2,256]{1,0:T(2,128)}, f32[2,256]{1,0:T(2,128)}, f32[2,256]{1,0:T(2,128)}, f32[2,256]{1,0:T(2,128)}, /*index=5*/f32[2,256]{1,0:T(2,128)}) all-reduce(bf16[2,256]{1,0:T(2,128)(2,1)S(1)} %copy.164, bf16[2,256]{1,0:T(2,128)(2,1)S(1)} %copy.166, ...), channel_id=1, replica_groups=mesh['fsdp'=4,'ctx'=2,'tp'=4] {'ctx','tp'}, use_global_device_ids=true, to_apply=%region_73.74 | all-reduce | flops 3072 | bytes 18432 | tf_op jit(solution)/shard_map/psum | solution.py:381
  1764.0 63.7 %all-reduce.5.cloned.1.call-done = (bf16[2,256,3,256]{3,1,2,0:T(8,128)(2,1)}, bf16[2,256,256]{2,1,0:T(8,128)(2,1)}, bf16[2,256,1024]{2,1,0:T(8,128)(2,1)}, bf16[2,1024,256]{2,1,0:T(8,128)(2,1)}) async-done(((bf16[2,256,3,256]{3,1,2,0:T(8,128)(2,1)}, bf16[2,256,256]{2,1,0:T(8,128)(2,1)}, bf16[2,256,1024]{2,1,0:T(8,128)(2,1)}, bf16[2,1024,256]{2,1,0:T(8,128)(2,1)}), (bf16[2,256,3,256]{3,1,2,0:T(8,128)(2,1)}, ...) | async-done | bytes 3145744 | tf_op jit(solution)/shard_map/psum | solution.py:373
  (757 shorter events, 621.2 us)
Async XLA Ops:
  7.2 73.7 %all-gather.55.cloned.1.call-start = ((), (), s32[]{:S(2)}) async-start(), calls=%async_computation.37 | async-start | bytes 1310720 | tf_op jit(solution)/shard_map/all_gather | solution.py:49
  33.4 60.4 %all-gather.83.cloned.1.call-start = ((), (), s32[]{:S(2)}) async-start(), calls=%async_computation.79 | async-start | bytes 1966080 | tf_op jit(solution)/shard_map/all_gather | solution.py:87
  34.5 112.5 %reduce-scatter.56.cloned.1.call-start = ((), (), s32[]{:S(2)}) async-start(), calls=%async_computation.38 | async-start | bytes 1310720 | tf_op jit(solution)/shard_map/reduce_scatter | solution.py:57
  149.2 71.2 %reduce-scatter.64.cloned.1.call-start = ((), (), s32[]{:S(2)}) async-start(), calls=%async_computation.46 | async-start | bytes 1310720 | tf_op jit(solution)/shard_map/reduce_scatter | solution.py:57
  195.4 73.3 %all-gather.85.cloned.1.call-start = ((), (), s32[]{:S(2)}) async-start(), calls=%async_computation.80 | async-start | bytes 2621440 | tf_op jit(solution)/shard_map/all_gather | solution.py:94
  197.7 88.6 %all-gather.65.cloned.1.call-start = ((), (), s32[]{:S(2)}) async-start(), calls=%async_computation.47 | async-start | bytes 1310720 | tf_op jit(solution)/shard_map/all_gather | solution.py:49
  225.0 80.2 %all-gather.57.cloned.1.call-start = ((), (), s32[]{:S(2)}) async-start(), calls=%async_computation.39 | async-start | bytes 1310720 | tf_op jit(solution)/shard_map/all_gather | solution.py:49
  225.7 127.9 %all-gather.87.cloned.1.call-start = ((), (), s32[]{:S(2)}) async-start(), calls=%async_computation.81 | async-start | bytes 2621440 | tf_op jit(solution)/shard_map/all_gather | solution.py:96
  226.9 161.3 %reduce-scatter.58.cloned.1.call-start = ((), (), s32[]{:S(2)}) async-start(), calls=%async_computation.40 | async-start | bytes 1310720 | tf_op jit(solution)/shard_map/reduce_scatter | solution.py:57
  361.7 99.1 %all-gather.89.cloned.1.call-start = ((), (), s32[]{:S(2)}) async-start(), calls=%async_computation.82 | async-start | bytes 1966080 | tf_op jit(solution)/shard_map/all_gather | solution.py:87
  362.7 110.7 %all-gather.67.cloned.1.call-start = ((), (), s32[]{:S(2)}) async-start(), calls=%async_computation.49 | async-start | bytes 1310720 | tf_op jit(solution)/shard_map/all_gather | solution.py:49
  411.2 80.4 %all-gather.59.cloned.1.call-start = ((), (), s32[]{:S(2)}) async-start(), calls=%async_computation.41 | async-start | bytes 1310720 | tf_op jit(solution)/shard_map/all_gather | solution.py:49
  411.8 164.8 %reduce-scatter.68.cloned.1.call-start = ((), (), s32[]{:S(2)}) async-start(), calls=%async_computation.50 | async-start | bytes 1310720 | tf_op jit(solution)/shard_map/reduce_scatter | solution.py:57
  547.9 76.7 %all-gather.91.cloned.1.call-start = ((), (), s32[]{:S(2)}) async-start(), calls=%async_computation.83 | async-start | bytes 2621440 | tf_op jit(solution)/shard_map/all_gather | solution.py:94
  548.5 93.2 %all-gather.69.cloned.1.call-start = ((), (), s32[]{:S(2)}) async-start(), calls=%async_computation.51 | async-start | bytes 1310720 | tf_op jit(solution)/shard_map/all_gather | solution.py:49
  579.4 81.2 %all-gather.61.cloned.1.call-start = ((), (), s32[]{:S(2)}) async-start(), calls=%async_computation.43 | async-start | bytes 1310720 | tf_op jit(solution)/shard_map/all_gather | solution.py:49
  580.2 98.6 %all-gather.97.cloned.1.call-start = ((), (), s32[]{:S(2)}) async-start(), calls=%async_computation.86 | async-start | bytes 1310720 | tf_op jit(solution)/shard_map/all_gather | solution.py:53
  582.1 145.1 %all-gather.93.cloned.1.call-start = ((), (), s32[]{:S(2)}) async-start(), calls=%async_computation.84 | async-start | bytes 2621440 | tf_op jit(solution)/shard_map/all_gather | solution.py:96
  582.8 160.9 %all-gather.95.cloned.1.call-start = ((), (), s32[]{:S(2)}) async-start(), calls=%async_computation.85 | async-start | bytes 1310720 | tf_op jit(solution)/shard_map/all_gather | solution.py:53
  583.6 188.3 %reduce-scatter.88.cloned.1.call-start = ((), (), s32[]{:S(2)}) async-start(), calls=%async_computation.64 | async-start | bytes 1310720 | tf_op jit(solution)/shard_map/reduce_scatter | solution.py:63
  736.3 62.4 %reduce-scatter.72.cloned.1.call-start = ((), (), s32[]{:S(2)}) async-start(), calls=%async_computation.53 | async-start | bytes 1310720 | tf_op jit(solution)/shard_map/reduce_scatter | solution.py:63
  752.3 73.9 %reduce-scatter.62.cloned.1.call-start = ((), (), s32[]{:S(2)}) async-start(), calls=%async_computation.44 | async-start | bytes 1310720 | tf_op jit(solution)/shard_map/reduce_scatter | solution.py:57
  756.7 96.9 %reduce-scatter.70.cloned.1.call-start = ((), (), s32[]{:S(2)}) async-start(), calls=%async_computation.52 | async-start | bytes 1310720 | tf_op jit(solution)/shard_map/reduce_scatter | solution.py:57
  760.9 113.2 %all-gather.77.cloned.1.call-start = ((), (), s32[]{:S(2)}) async-start(), calls=%async_computation.65 | async-start | bytes 1310720 | tf_op jit(solution)/shard_map/all_gather | solution.py:53
  858.0 115.2 %reduce-scatter.90.cloned.1.call-start = ((), (), s32[]{:S(2)}) async-start(), calls=%async_computation.66 | async-start | bytes 786432 | tf_op jit(solution)/shard_map/reduce_scatter | solution.py:232
  906.5 66.7 %reduce-scatter.92.cloned.1.call-start = ((), (), s32[]{:S(2)}) async-start(), calls=%async_computation.67 | async-start | bytes 786432 | tf_op jit(solution)/shard_map/reduce_scatter | solution.py:235
  915.1 83.7 %reduce-scatter.74.cloned.1.call-start = ((), (), s32[]{:S(2)}) async-start(), calls=%async_computation.55 | async-start | bytes 786432 | tf_op jit(solution)/shard_map/reduce_scatter | solution.py:232
  1037.5 62.4 %reduce-scatter.96.cloned.1.call-start = ((), (), s32[]{:S(2)}) async-start(), calls=%async_computation.70 | async-start | bytes 1310720 | tf_op jit(solution)/shard_map/reduce_scatter | solution.py:63
  1062.3 65.7 %reduce-scatter.80.cloned.1.call-start = ((), (), s32[]{:S(2)}) async-start(), calls=%async_computation.59 | async-start | bytes 1310720 | tf_op jit(solution)/shard_map/reduce_scatter | solution.py:63
  1081.1 69.0 %all-gather.81.cloned.1.call-start = ((), (), s32[]{:S(2)}) async-start(), calls=%async_computation.71 | async-start | bytes 1310720 | tf_op jit(solution)/shard_map/all_gather | solution.py:53
  1135.2 113.6 %reduce-scatter.98.cloned.1.call-start = ((), (), s32[]{:S(2)}) async-start(), calls=%async_computation.72 | async-start | bytes 786432 | tf_op jit(solution)/shard_map/reduce_scatter | solution.py:232
  1182.3 66.5 %reduce-scatter.100.cloned.1.call-start = ((), (), s32[]{:S(2)}) async-start(), calls=%async_computation.73 | async-start | bytes 786432 | tf_op jit(solution)/shard_map/reduce_scatter | solution.py:235
  1190.5 84.3 %reduce-scatter.82.cloned.1.call-start = ((), (), s32[]{:S(2)}) async-start(), calls=%async_computation.61 | async-start | bytes 786432 | tf_op jit(solution)/shard_map/reduce_scatter | solution.py:232
  1226.4 94.5 %reduce-scatter.102.cloned.1.call-start = ((), (), s32[]{:S(2)}) async-start(), calls=%async_computation.74 | async-start | bytes 1310720 | tf_op jit(solution)/shard_map/reduce_scatter | solution.py:63
  1252.5 68.5 %reduce-scatter.86.cloned.1.call-start = ((), (), s32[]{:S(2)}) async-start(), calls=%async_computation.63 | async-start | bytes 1310720 | tf_op jit(solution)/shard_map/reduce_scatter | solution.py:63
  1283.2 132.0 %reduce-scatter.110.cloned.1.call-start = ((), (), s32[]{:S(2)}) async-start(), calls=%async_computation.78 | async-start | bytes 5242880 | tf_op jit(solution)/shard_map/reduce_scatter | solution.py:365
  1293.4 201.3 %reduce-scatter.108.cloned.1.call-start = ((), (), s32[]{:S(2)}) async-start(), calls=%async_computation.77 | async-start | bytes 5242880 | tf_op jit(solution)/shard_map/reduce_scatter | solution.py:359
  1303.4 254.6 %reduce-scatter.104.cloned.1.call-start = ((), (), s32[]{:S(2)}) async-start(), calls=%async_computation.75 | async-start | bytes 3932160 | tf_op jit(solution)/shard_map/reduce_scatter | solution.py:338
  1312.7 267.0 %reduce-scatter.128.cloned.1.call-start = ((), (), s32[]{:S(2)}) async-start(), calls=%async_computation.95 | async-start | bytes 327680
  1314.8 284.5 %reduce-scatter.126.cloned.1.call-start = ((), (), s32[]{:S(2)}) async-start(), calls=%async_computation.94 | async-start | bytes 20480
  1315.8 303.4 %reduce-scatter.124.cloned.1.call-start = ((), (), s32[]{:S(2)}) async-start(), calls=%async_computation.93 | async-start | bytes 327680
  1316.8 322.7 %reduce-scatter.122.cloned.1.call-start = ((), (), s32[]{:S(2)}) async-start(), calls=%async_computation.92 | async-start | bytes 327680
  1317.8 341.9 %reduce-scatter.120.cloned.1.call-start = ((), (), s32[]{:S(2)}) async-start(), calls=%async_computation.91 | async-start | bytes 327680
  1318.7 361.0 %reduce-scatter.116.cloned.1.call-start = ((), (), s32[]{:S(2)}) async-start(), calls=%async_computation.89 | async-start | bytes 20480
  1319.7 379.4 %reduce-scatter.118.cloned.1.call-start = ((), (), s32[]{:S(2)}) async-start(), calls=%async_computation.90 | async-start | bytes 20480
  1320.9 398.8 %reduce-scatter.114.cloned.1.call-start = ((), (), s32[]{:S(2)}) async-start(), calls=%async_computation.88 | async-start | bytes 327680
  1325.1 415.2 %reduce-scatter.112.cloned.1.call-start = ((), (), s32[]{:S(2)}) async-start(), calls=%async_computation.87 | async-start | bytes 327680
  1326.1 501.6 %all-reduce.5.cloned.1.call-start = ((), (), s32[]{:S(2)}) async-start(), calls=%async_computation.96 | async-start | bytes 6291456 | tf_op jit(solution)/shard_map/psum | solution.py:373
  (162 other events, 3449.6 us)
Sparse Core Ops, SparseCore 0:
  52.1 41.7 all-gather.82
  121.3 25.6 reduce-scatter.55
  149.3 16.7 all-gather.62
  195.5 24.8 reduce-scatter.63
  222.4 46.2 all-gather.84
  288.5 16.7 all-gather.56
  307.4 46.2 all-gather.86
  357.6 23.1 reduce-scatter.57
  383.4 24.8 reduce-scatter.65
  410.3 44.1 all-gather.88
  456.7 16.7 all-gather.66
  474.9 16.7 all-gather.58
  523.5 24.8 reduce-scatter.67
  551.5 24.9 reduce-scatter.59
  578.5 46.1 all-gather.90
  643.8 16.7 all-gather.60
  662.0 16.7 all-gather.96
  680.9 46.2 all-gather.92
  746.3 24.8 reduce-scatter.87
  773.7 24.8 reduce-scatter.71
  801.2 24.9 reduce-scatter.61
  828.7 24.8 reduce-scatter.69
  857.4 16.7 all-gather.76
  875.7 16.7 all-gather.70
  979.3 25.0 reduce-scatter.93
  1007.1 24.8 reduce-scatter.77
  1037.0 16.7 all-gather.78
  1055.8 16.7 all-gather.72
  1074.9 24.8 reduce-scatter.95
  1103.1 24.9 reduce-scatter.79
  1133.3 16.7 all-gather.80
  1152.2 16.7 all-gather.74
  1255.3 24.8 reduce-scatter.101
  1283.3 24.9 reduce-scatter.85
  1310.4 27.1 reduce-scatter.105
  1339.8 75.4 reduce-scatter.109
  1417.4 77.2 reduce-scatter.107
  1497.1 60.7 reduce-scatter.103
  1560.1 19.5 reduce-scatter.127
  1582.0 17.1 reduce-scatter.125
  1601.4 17.7 reduce-scatter.123
  1621.5 17.9 reduce-scatter.121
  1641.8 17.7 reduce-scatter.119
  1662.5 17.1 reduce-scatter.115
  1682.0 17.0 reduce-scatter.117
  1701.8 17.8 reduce-scatter.113
  1722.4 17.7 reduce-scatter.111
  1742.7 84.8 all-reduce.4
  (12 shorter events, 178.4 us)
where the time goes:
time: 1850 us; the launch traced here: 1840 us
  waiting for transfers between devices  986 us (53%)
  matrix products  382 us (21%)
  blocking collectives  331 us (18%)
  other arithmetic  66.7 us (4%)
  local copies, waits for them, and re-layouts  54.1 us (3%)
    unnamed x69, waiting for transfers between devices  168 us
    all_gather x8, waiting for transfers between devices, spread_rows(): return lax.all_gather(rows, 'tp', axis=0, tiled=True)  106 us
    reduce_scatter x8, waiting for transfers between devices, combine_grads(): lax.psum_scatter(partial_value.astype(jnp.bfloat16), 'tp', scatter_dimens...  103 us
    reduce_scatter x8, waiting for transfers between devices, combine_rows(): lax.psum_scatter(partial_value.astype(jnp.bfloat16), 'tp', scatter_dimens...  92.7 us
    dot_general x4, matrix products, backward_layer(): jnp.einsum('hqk,hqd->hkd', d_raw, query_heads, preferred_element_type=jnp...  89.9 us
    dot_general x4, matrix products, backward_layer(): jnp.einsum('hqk,hkd->hqd', d_raw, key_heads, preferred_element_type=jnp.f...  87.6 us
    all_gather x2, waiting for transfers between devices, fetch(): lax.all_gather(reduce_weight[layer_id], 'fsdp', axis=1, tiled=True)  83.4 us
    reduce_scatter x1, waiting for transfers between devices, local(): lax.psum_scatter(stacked[9].astype(jnp.bfloat16), 'fsdp', scatter_dimensi...  79.5 us
  transfers between devices with their start and end apart: 60, of which 42 were waited for; matrix products, arithmetic and copies ran while one was open for 23% of the time, Pallas kernels for 0%

commit v1 on v0

--- a/solution.py
+++ b/solution.py
@@ -10,6 +10,16 @@
 masked_score = -10000.0
 
 
+def ring_gather(x, axis, dim):
+    ways, here, step = (lax.axis_size(axis), lax.axis_index(axis), x.shape[dim])
+    lengths = [n * ways if d == dim else n for d, n in enumerate(x.shape)]
+    full = lax.dynamic_update_slice_in_dim(jnp.zeros(lengths, x.dtype), x, here * step, axis=dim)
+    for far in range(1, ways):
+        x = lax.ppermute(x, axis, [(d, (d + 1) % ways) for d in range(ways)])
+        full = lax.dynamic_update_slice_in_dim(full, x, (here - far) % ways * step, axis=dim)
+    return full
+
+
 def norm_rows(rows, gain, shift):
     middle = jnp.mean(rows, axis=-1, keepdims=True)
     centred = rows - middle
@@ -46,7 +56,7 @@
 
 
 def spread_rows(rows):
-    return lax.all_gather(rows, "tp", axis=0, tiled=True)
+    return ring_gather(rows, "tp", 0)
 
 
 def gather_grad(rows):

time: 1850 us -> 1750 us (0.946)
  waiting for transfers between devices: 986 us -> 844 us
  local copies, waits for them, and re-layouts: 54.1 us -> 105 us
    all_gather x8 -> x0, waiting for transfers between devices: 106 us -> none  [spread_rows(): return lax.all_gather(rows, 'tp', axis=0, tiled=True)]
    all_gather x2, waiting for transfers between devices: 55.2 us -> 17.6 us  [fetch(): lax.all_gather(expand_weight[layer_id], 'fsdp', axis=0, tiled=True)]
    ppermute x0 -> x24, waiting for transfers between devices: none -> 28.7 us  [ring_gather(): x = lax.ppermute(x, axis, [(d, (d + 1) % ways) for d in range(ways)])]
    ppermute x0 -> x24, local copies, waits for them, and re-layouts: none -> 20.6 us  [ring_gather(): x = lax.ppermute(x, axis, [(d, (d + 1) % ways) for d in range(ways)])]
    unnamed x69 -> x61, waiting for transfers between devices: 168 us -> 166 us
  transfers between devices with their start and end apart: 60 -> 76, of which waited for: 42 -> 45; matrix products, arithmetic and copies ran while one was open for 23% -> 27% of each run, Pallas kernels for 0% -> 0%
where the time goes in v1:
time: 1750 us; the launch traced here: 1740 us
  waiting for transfers between devices  844 us (48%)
  matrix products  375 us (21%)
  blocking collectives  327 us (19%)
  local copies, waits for them, and re-layouts  105 us (6%)
  other arithmetic  60.4 us (3%)
  between operations  18.4 us (1%)
    unnamed x61, waiting for transfers between devices  166 us
    reduce_scatter x8, waiting for transfers between devices, combine_grads(): lax.psum_scatter(partial_value.astype(jnp.bfloat16), 'tp', scatter_dimens...  102 us
    reduce_scatter x8, waiting for transfers between devices, combine_rows(): lax.psum_scatter(partial_value.astype(jnp.bfloat16), 'tp', scatter_dimens...  94.2 us
    dot_general x4, matrix products, backward_layer(): jnp.einsum('hqk,hkd->hqd', d_raw, key_heads, preferred_element_type=jnp.f...  88.6 us
    dot_general x4, matrix products, backward_layer(): jnp.einsum('hqk,hqd->hkd', d_raw, query_heads, preferred_element_type=jnp...  86.5 us
    reduce_scatter x1, waiting for transfers between devices, local(): lax.psum_scatter(stacked[9].astype(jnp.bfloat16), 'fsdp', scatter_dimensi...  79.6 us
    all_gather x2, waiting for transfers between devices, fetch(): lax.all_gather(reduce_weight[layer_id], 'fsdp', axis=1, tiled=True)  78.8 us
    reduce_scatter x1, waiting for transfers between devices, local(): lax.psum_scatter(stacked[11].astype(jnp.bfloat16), 'fsdp', scatter_dimens...  77.9 us
  transfers between devices with their start and end apart: 76, of which 45 were waited for; matrix products, arithmetic and copies ran while one was open for 27% of the time, Pallas kernels for 0%

profile of v1, /device:TPU:0, one launch (start us, length us, event | category | flops | bytes accessed | tf_op | source)
XLA Modules:
  0.0 1739.5 jit_solution(2099537712184992757)
XLA Ops:
  10.8 12.6 all-gather
  38.1 20.7 %all-gather.6 = bf16[1,256,1024]{2,1,0:T(8,128)(2,1)S(1)} all-gather(bf16[1,256,256]{2,1,0:T(8,128)(2,1)S(1)} %get-tuple-element.130), channel_id=8, replica_groups=mesh['fsdp'=4,'ctx'=2,'tp'=4] {'fsdp'}, dimensions={2}, use_global_device_ids=true | all-gather | bytes 655360 | tf_op jit(solution)/shard_map/all_gather | solution.py:100
  59.4 13.1 all-gather.3
  73.4 13.1 all-gather.5
  127.0 15.0 reduce-scatter.56.cloned.1.call-done
  190.2 11.1 all-gather.8
  221.6 13.6 all-gather.11
  267.8 11.7 multiply_convert_fusion.7
  279.5 31.0 %all-gather.63.cloned.1.call-done = bf16[1,1024,1024]{2,1,0:T(8,128)(2,1)} async-done(((bf16[1,1024,256]{2,1,0:T(8,128)(2,1)}), bf16[1,1024,1024]{2,1,0:T(8,128)(2,1)}) %all-gather.63.cloned.1.call-update) | async-done | bytes 2097168 | tf_op jit(solution)/shard_map/all_gather | solution.py:106
  345.2 20.4 %reduce-scatter.66.cloned.1.call-done = bf16[128,1024]{1,0:T(8,128)(2,1)} async-done(((bf16[512,1024]{1,0:T(8,128)(2,1)}), bf16[128,1024]{1,0:T(8,128)(2,1)}) %reduce-scatter.66.cloned.1.call-update) | async-done | bytes 262160 | tf_op jit(solution)/shard_map/reduce_scatter | solution.py:67
  368.0 13.2 all-gather.17
  381.4 13.9 all-gather.19
  395.5 20.2 %all-gather.20 = bf16[1,256,1024]{2,1,0:T(8,128)(2,1)S(1)} all-gather(bf16[1,256,256]{2,1,0:T(8,128)(2,1)S(1)} %copy-done.88), channel_id=22, replica_groups=mesh['fsdp'=4,'ctx'=2,'tp'=4] {'fsdp'}, dimensions={2}, use_global_device_ids=true | all-gather | bytes 655360 | tf_op jit(solution)/shard_map/all_gather | solution.py:100
  490.8 11.1 all-gather.21
  522.1 13.3 all-gather.25
  570.9 13.0 multiply_convert_fusion.6
  583.9 47.7 %all-gather.69.cloned.1.call-done = bf16[1,1024,1024]{2,1,0:T(8,128)(2,1)} async-done(((bf16[1,1024,256]{2,1,0:T(8,128)(2,1)}), bf16[1,1024,1024]{2,1,0:T(8,128)(2,1)}) %all-gather.69.cloned.1.call-update) | async-done | bytes 2097168 | tf_op jit(solution)/shard_map/all_gather | solution.py:106
  665.8 10.9 all-gather.27
  676.6 26.2 %reduce-scatter.72.cloned.1.call-done = bf16[128,1024]{1,0:T(8,128)(2,1)} async-done(((bf16[512,1024]{1,0:T(8,128)(2,1)}), bf16[128,1024]{1,0:T(8,128)(2,1)}) %reduce-scatter.72.cloned.1.call-update) | async-done | bytes 262160 | tf_op jit(solution)/shard_map/reduce_scatter | solution.py:73
  704.3 25.8 %reduce-scatter.62.cloned.1.call-done = bf16[128,1024]{1,0:T(8,128)(2,1)} async-done(((bf16[512,1024]{1,0:T(8,128)(2,1)}), bf16[128,1024]{1,0:T(8,128)(2,1)}) %reduce-scatter.62.cloned.1.call-update) | async-done | bytes 262160 | tf_op jit(solution)/shard_map/reduce_scatter | solution.py:67
  730.1 27.5 %reduce-scatter.70.cloned.1.call-done = bf16[128,1024]{1,0:T(8,128)(2,1)} async-done(((bf16[512,1024]{1,0:T(8,128)(2,1)}), bf16[128,1024]{1,0:T(8,128)(2,1)}) %reduce-scatter.70.cloned.1.call-update) | async-done | bytes 262160 | tf_op jit(solution)/shard_map/reduce_scatter | solution.py:67
  762.5 16.2 all-gather.53.cloned.1.call-done
  785.0 22.3 %fusion.221 = bf16[4,1024,64]{1,2,0:T(8,128)(2,1)S(1)} fusion(f32[4,512,1024]{2,1,0:T(8,128)} %fusion.467, f32[4,512,1024]{2,1,0:T(8,128)} %copy-done.5, f32[4,512]{1,0:T(4,128)S(1)} %log_add_fusion.1, f32[1024]{0:T(1024)S(1)} %bitcast.661, f32[512,4,64]{0,2,1:T(8,128)S(1)} %bitcast.579, f32[4,64]{1,0:T(4,128)S(1)} %copy.236), kind=kOutput, calls=%fused_computation.234 | convolution fusion | flops 292031488 | bytes 17839104 | tf_op jit(solution)/shard_map/hqk,hqd->hkd/dot_general | solution.py:238
  821.2 22.4 %fusion.227 = bf16[4,1024,64]{1,2,0:T(8,128)(2,1)S(1)} fusion(f32[4,512,1024]{2,1,0:T(8,128)} %fusion.465, f32[4,512,1024]{2,1,0:T(8,128)} %copy-done.4, f32[4,512]{1,0:T(4,128)S(1)} %log_add_fusion.3, f32[1024]{0:T(1024)S(1)} %bitcast.649, f32[512,4,64]{0,2,1:T(8,128)S(1)} %bitcast.577, f32[4,64]{1,0:T(4,128)S(1)} %copy.236), kind=kOutput, calls=%fused_computation.236 | convolution fusion | flops 292031488 | bytes 17839104 | tf_op jit(solution)/shard_map/hqk,hqd->hkd/dot_general | solution.py:238
  851.1 22.3 %convert_reduce_fusion.26 = (f32[4,64]{1,0:T(4,128)}, bf16[4,512,64]{1,2,0:T(8,128)(2,1)S(1)}) fusion(bf16[4,1024,64]{1,2,0:T(8,128)(2,1)S(1)} %bitcast.575, f32[4,512,1024]{2,1,0:T(8,128)} %fusion.467, f32[4,512,1024]{2,1,0:T(8,128)} %copy-done.5, f32[4,512]{1,0:T(4,128)S(1)} %log_add_fusion.1, f32[1024]{0:T(1024)S(1)} %bitcast.663), kind=kOutput, calls=%fused_computation.405 | convolution fusion | flops 291900160 | bytes 17576960 | tf_op jit(solution)/shard_map/hqk,hkd->hqd/dot_general | solution.py:236
  877.5 22.4 %convert_reduce_fusion.27 = (f32[4,64]{1,0:T(4,128)}, bf16[4,512,64]{1,2,0:T(8,128)(2,1)S(1)}) fusion(bf16[4,1024,64]{1,2,0:T(8,128)(2,1)S(1)} %bitcast.573, f32[4,512,1024]{2,1,0:T(8,128)} %fusion.465, f32[4,512,1024]{2,1,0:T(8,128)} %copy-done.4, f32[4,512]{1,0:T(4,128)S(1)} %log_add_fusion.3, f32[1024]{0:T(1024)S(1)} %bitcast.651), kind=kOutput, calls=%fused_computation.406 | convolution fusion | flops 291900160 | bytes 17576960 | tf_op jit(solution)/shard_map/hqk,hkd->hqd/dot_general | solution.py:236
  904.4 27.5 %reduce-scatter.78.cloned.1.call-done = bf16[128,1024]{1,0:T(8,128)(2,1)} async-done(((bf16[512,1024]{1,0:T(8,128)(2,1)}), bf16[128,1024]{1,0:T(8,128)(2,1)}) %reduce-scatter.78.cloned.1.call-update) | async-done | bytes 262160 | tf_op jit(solution)/shard_map/reduce_scatter | solution.py:73
  937.3 16.1 all-gather.55.cloned.1.call-done
  980.5 19.9 %reduce-scatter.96.cloned.1.call-done = bf16[128,1024]{1,0:T(8,128)(2,1)} async-done(((bf16[512,1024]{1,0:T(8,128)(2,1)}), bf16[128,1024]{1,0:T(8,128)(2,1)}) %reduce-scatter.96.cloned.1.call-update) | async-done | bytes 262160 | tf_op jit(solution)/shard_map/reduce_scatter | solution.py:73
  1000.4 28.0 %reduce-scatter.80.cloned.1.call-done = bf16[128,1024]{1,0:T(8,128)(2,1)} async-done(((bf16[512,1024]{1,0:T(8,128)(2,1)}), bf16[128,1024]{1,0:T(8,128)(2,1)}) %reduce-scatter.80.cloned.1.call-update) | async-done | bytes 262160 | tf_op jit(solution)/shard_map/reduce_scatter | solution.py:73
  1034.6 15.9 all-gather.57.cloned.1.call-done
  1056.9 19.0 %fusion.218 = bf16[4,1024,64]{1,2,0:T(8,128)(2,1)} fusion(f32[4,512,1024]{2,1,0:T(8,128)} %fusion.468, f32[4,512,1024]{2,1,0:T(8,128)} %copy-done.3, f32[4,512]{1,0:T(4,128)S(1)} %log_add_fusion, f32[1024]{0:T(1024)S(1)} %bitcast.664, f32[512,4,64]{0,2,1:T(8,128)} %bitcast.569, f32[4,64]{1,0:T(4,128)S(1)} %copy-done.122), kind=kOutput, calls=%fused_computation.233 | convolution fusion | flops 292031488 | bytes 17839104 | tf_op jit(solution)/shard_map/hqk,hqd->hkd/dot_general | solution.py:238
  1092.7 22.9 %fusion.224 = bf16[4,1024,64]{1,2,0:T(8,128)(2,1)} fusion(f32[4,512,1024]{2,1,0:T(8,128)} %fusion.466, f32[4,512,1024]{2,1,0:T(8,128)} %copy-done.2, f32[4,512]{1,0:T(4,128)S(1)} %log_add_fusion.2, f32[1024]{0:T(1024)S(1)} %bitcast.652, f32[512,4,64]{0,2,1:T(8,128)S(1)} %bitcast.563, f32[4,64]{1,0:T(4,128)S(1)} %copy-done.122), kind=kOutput, calls=%fused_computation.235 | convolution fusion | flops 292031488 | bytes 17839104 | tf_op jit(solution)/shard_map/hqk,hqd->hkd/dot_general | solution.py:238
  1125.9 22.2 %convert_reduce_fusion.28 = (f32[4,64]{1,0:T(4,128)S(1)}, bf16[4,512,64]{1,2,0:T(8,128)(2,1)}) fusion(bf16[4,1024,64]{1,2,0:T(8,128)(2,1)S(1)} %bitcast.567, f32[4,512,1024]{2,1,0:T(8,128)} %fusion.468, f32[4,512,1024]{2,1,0:T(8,128)} %copy-done.3, f32[4,512]{1,0:T(4,128)S(1)} %log_add_fusion, f32[1024]{0:T(1024)S(1)} %bitcast.666), kind=kOutput, calls=%fused_computation.407 | convolution fusion | flops 291900160 | bytes 17576960 | tf_op jit(solution)/shard_map/hqk,hkd->hqd/dot_general | solution.py:236
  1153.2 21.6 %convert_reduce_fusion.29 = (f32[4,64]{1,0:T(4,128)S(1)}, bf16[4,512,64]{1,2,0:T(8,128)(2,1)S(1)}) fusion(bf16[4,1024,64]{1,2,0:T(8,128)(2,1)S(1)} %bitcast.561, f32[4,512,1024]{2,1,0:T(8,128)} %fusion.466, f32[4,512,1024]{2,1,0:T(8,128)} %copy-done.2, f32[4,512]{1,0:T(4,128)S(1)} %log_add_fusion.2, f32[1024]{0:T(1024)S(1)} %bitcast.654), kind=kOutput, calls=%fused_computation.408 | convolution fusion | flops 291900160 | bytes 17576960 | tf_op jit(solution)/shard_map/hqk,hkd->hqd/dot_general | solution.py:236
  1235.5 77.9 %reduce-scatter.110.cloned.1.call-done = bf16[2,1024,256]{2,1,0:T(8,128)(2,1)} async-done(((bf16[2,1024,1024]{2,1,0:T(8,128)(2,1)}), bf16[2,1024,256]{2,1,0:T(8,128)(2,1)}) %reduce-scatter.110.cloned.1.call-update) | async-done | bytes 1048592 | tf_op jit(solution)/shard_map/reduce_scatter | solution.py:375
  1313.4 79.6 %reduce-scatter.108.cloned.1.call-done = bf16[2,256,1024]{2,1,0:T(8,128)(2,1)} async-done(((bf16[2,1024,1024]{2,1,0:T(8,128)(2,1)}), bf16[2,256,1024]{2,1,0:T(8,128)(2,1)}) %reduce-scatter.108.cloned.1.call-update) | async-done | bytes 1048592 | tf_op jit(solution)/shard_map/reduce_scatter | solution.py:369
  1393.0 63.2 %reduce-scatter.104.cloned.1.call-done = bf16[2,256,3,256]{3,1,2,0:T(8,128)(2,1)} async-done(((bf16[2,1024,3,256]{3,1,2,0:T(8,128)(2,1)}), bf16[2,256,3,256]{3,1,2,0:T(8,128)(2,1)}) %reduce-scatter.104.cloned.1.call-update) | async-done | bytes 786448 | tf_op jit(solution)/shard_map/reduce_scatter | solution.py:348
  1458.1 20.0 %reduce-scatter.128.cloned.1.call-done = bf16[256,2]{1,0:T(8,128)(2,1)} async-done(((bf16[1024,2]{1,0:T(8,128)(2,1)}), bf16[256,2]{1,0:T(8,128)(2,1)}) %reduce-scatter.128.cloned.1.call-update) | async-done | bytes 1040
  1479.0 18.5 %reduce-scatter.126.cloned.1.call-done = bf16[16,32]{1,0:T(8,128)(2,1)} async-done(((bf16[64,32]{1,0:T(8,128)(2,1)}), bf16[16,32]{1,0:T(8,128)(2,1)}) %reduce-scatter.126.cloned.1.call-update) | async-done | bytes 1040
  1498.3 19.2 %reduce-scatter.124.cloned.1.call-done = bf16[256,2]{1,0:T(8,128)(2,1)} async-done(((bf16[1024,2]{1,0:T(8,128)(2,1)}), bf16[256,2]{1,0:T(8,128)(2,1)}) %reduce-scatter.124.cloned.1.call-update) | async-done | bytes 1040
  1518.4 19.0 %reduce-scatter.122.cloned.1.call-done = bf16[256,2]{1,0:T(8,128)(2,1)} async-done(((bf16[1024,2]{1,0:T(8,128)(2,1)}), bf16[256,2]{1,0:T(8,128)(2,1)}) %reduce-scatter.122.cloned.1.call-update) | async-done | bytes 1040
  1538.4 19.9 %reduce-scatter.120.cloned.1.call-done = bf16[256,2]{1,0:T(8,128)(2,1)} async-done(((bf16[1024,2]{1,0:T(8,128)(2,1)}), bf16[256,2]{1,0:T(8,128)(2,1)}) %reduce-scatter.120.cloned.1.call-update) | async-done | bytes 1040
  1559.2 18.9 %reduce-scatter.116.cloned.1.call-done = bf16[16,8]{1,0:T(8,128)(2,1)} async-done(((bf16[64,8]{1,0:T(8,128)(2,1)}), bf16[16,8]{1,0:T(8,128)(2,1)}) %reduce-scatter.116.cloned.1.call-update) | async-done | bytes 272
  1579.0 18.4 %reduce-scatter.118.cloned.1.call-done = bf16[16,8]{1,0:T(8,128)(2,1)} async-done(((bf16[64,8]{1,0:T(8,128)(2,1)}), bf16[16,8]{1,0:T(8,128)(2,1)}) %reduce-scatter.118.cloned.1.call-update) | async-done | bytes 272
  1618.9 19.8 %reduce-scatter.112.cloned.1.call-done = bf16[256,2]{1,0:T(8,128)(2,1)} async-done(((bf16[1024,2]{1,0:T(8,128)(2,1)}), bf16[256,2]{1,0:T(8,128)(2,1)}) %reduce-scatter.112.cloned.1.call-update) | async-done | bytes 1040
  1639.6 22.8 %all-reduce = (f32[2,256]{1,0:T(2,128)}, f32[2,256]{1,0:T(2,128)}, f32[2,256]{1,0:T(2,128)}, f32[2,256]{1,0:T(2,128)}, f32[2,256]{1,0:T(2,128)}, /*index=5*/f32[2,256]{1,0:T(2,128)}) all-reduce(bf16[2,256]{1,0:T(2,128)(2,1)S(1)} %copy.292, bf16[2,256]{1,0:T(2,128)(2,1)S(1)} %copy.294, ...), channel_id=1, replica_groups=mesh['fsdp'=4,'ctx'=2,'tp'=4] {'ctx','tp'}, use_global_device_ids=true, to_apply=%region_73.74 | all-reduce | flops 3072 | bytes 18432 | tf_op jit(solution)/shard_map/psum | solution.py:391
  1662.4 63.6 %all-reduce.5.cloned.1.call-done = (bf16[2,256,3,256]{3,1,2,0:T(8,128)(2,1)}, bf16[2,256,256]{2,1,0:T(8,128)(2,1)}, bf16[2,256,1024]{2,1,0:T(8,128)(2,1)}, bf16[2,1024,256]{2,1,0:T(8,128)(2,1)}) async-done(((bf16[2,256,3,256]{3,1,2,0:T(8,128)(2,1)}, bf16[2,256,256]{2,1,0:T(8,128)(2,1)}, bf16[2,256,1024]{2,1,0:T(8,128)(2,1)}, bf16[2,1024,256]{2,1,0:T(8,128)(2,1)}), (bf16[2,256,3,256]{3,1,2,0:T(8,128)(2,1)}, ...) | async-done | bytes 3145744 | tf_op jit(solution)/shard_map/psum | solution.py:383
  (909 shorter events, 576.4 us)
Async XLA Ops:
  7.2 81.8 %all-gather.59.cloned.1.call-start = ((), (), s32[]{:S(2)}) async-start(), calls=%async_computation.71 | async-start | bytes 1966080 | tf_op jit(solution)/shard_map/all_gather | solution.py:97
  9.5 132.5 %reduce-scatter.56.cloned.1.call-start = ((), (), s32[]{:S(2)}) async-start(), calls=%async_computation.37 | async-start | bytes 1310720 | tf_op jit(solution)/shard_map/reduce_scatter | solution.py:67
  116.9 98.2 %reduce-scatter.64.cloned.1.call-start = ((), (), s32[]{:S(2)}) async-start(), calls=%async_computation.41 | async-start | bytes 1310720 | tf_op jit(solution)/shard_map/reduce_scatter | solution.py:67
  188.5 74.9 %all-gather.61.cloned.1.call-start = ((), (), s32[]{:S(2)}) async-start(), calls=%async_computation.72 | async-start | bytes 2621440 | tf_op jit(solution)/shard_map/all_gather | solution.py:104
  189.6 121.0 %all-gather.63.cloned.1.call-start = ((), (), s32[]{:S(2)}) async-start(), calls=%async_computation.73 | async-start | bytes 2621440 | tf_op jit(solution)/shard_map/all_gather | solution.py:106
  220.4 124.8 %reduce-scatter.58.cloned.1.call-start = ((), (), s32[]{:S(2)}) async-start(), calls=%async_computation.38 | async-start | bytes 1310720 | tf_op jit(solution)/shard_map/reduce_scatter | solution.py:67
  318.7 110.4 %all-gather.65.cloned.1.call-start = ((), (), s32[]{:S(2)}) async-start(), calls=%async_computation.74 | async-start | bytes 1966080 | tf_op jit(solution)/shard_map/all_gather | solution.py:97
  319.7 199.4 %reduce-scatter.68.cloned.1.call-start = ((), (), s32[]{:S(2)}) async-start(), calls=%async_computation.43 | async-start | bytes 1310720 | tf_op jit(solution)/shard_map/reduce_scatter | solution.py:67
  464.5 54.6 %reduce-scatter.60.cloned.1.call-start = ((), (), s32[]{:S(2)}) async-start(), calls=%async_computation.39 | async-start | bytes 1310720 | tf_op jit(solution)/shard_map/reduce_scatter | solution.py:67
  488.4 77.8 %all-gather.67.cloned.1.call-start = ((), (), s32[]{:S(2)}) async-start(), calls=%async_computation.75 | async-start | bytes 2621440 | tf_op jit(solution)/shard_map/all_gather | solution.py:104
  489.1 94.8 %all-gather.73.cloned.1.call-start = ((), (), s32[]{:S(2)}) async-start(), calls=%async_computation.78 | async-start | bytes 1310720 | tf_op jit(solution)/shard_map/all_gather | solution.py:63
  490.0 141.6 %all-gather.69.cloned.1.call-start = ((), (), s32[]{:S(2)}) async-start(), calls=%async_computation.76 | async-start | bytes 2621440 | tf_op jit(solution)/shard_map/all_gather | solution.py:106
  490.8 157.3 %all-gather.71.cloned.1.call-start = ((), (), s32[]{:S(2)}) async-start(), calls=%async_computation.77 | async-start | bytes 1310720 | tf_op jit(solution)/shard_map/all_gather | solution.py:63
  521.9 154.7 %reduce-scatter.88.cloned.1.call-start = ((), (), s32[]{:S(2)}) async-start(), calls=%async_computation.56 | async-start | bytes 1310720 | tf_op jit(solution)/shard_map/reduce_scatter | solution.py:73
  640.2 62.6 %reduce-scatter.72.cloned.1.call-start = ((), (), s32[]{:S(2)}) async-start(), calls=%async_computation.45 | async-start | bytes 1310720 | tf_op jit(solution)/shard_map/reduce_scatter | solution.py:73
  656.6 73.5 %reduce-scatter.62.cloned.1.call-start = ((), (), s32[]{:S(2)}) async-start(), calls=%async_computation.40 | async-start | bytes 1310720 | tf_op jit(solution)/shard_map/reduce_scatter | solution.py:67
  661.1 96.5 %reduce-scatter.70.cloned.1.call-start = ((), (), s32[]{:S(2)}) async-start(), calls=%async_computation.44 | async-start | bytes 1310720 | tf_op jit(solution)/shard_map/reduce_scatter | solution.py:67
  665.7 113.0 %all-gather.53.cloned.1.call-start = ((), (), s32[]{:S(2)}) async-start(), calls=%async_computation.57 | async-start | bytes 1310720 | tf_op jit(solution)/shard_map/all_gather | solution.py:63
  761.9 53.1 %all-gather.47.cloned.1.call-start = ((), (), s32[]{:S(2)}) async-start(), calls=%async_computation.46 | async-start | bytes 1310720 | tf_op jit(solution)/shard_map/all_gather | solution.py:63
  762.5 111.1 %reduce-scatter.90.cloned.1.call-start = ((), (), s32[]{:S(2)}) async-start(), calls=%async_computation.58 | async-start | bytes 786432 | tf_op jit(solution)/shard_map/reduce_scatter | solution.py:242
  808.4 65.2 %reduce-scatter.92.cloned.1.call-start = ((), (), s32[]{:S(2)}) async-start(), calls=%async_computation.59 | async-start | bytes 786432 | tf_op jit(solution)/shard_map/reduce_scatter | solution.py:245
  814.7 85.4 %reduce-scatter.74.cloned.1.call-start = ((), (), s32[]{:S(2)}) async-start(), calls=%async_computation.47 | async-start | bytes 786432 | tf_op jit(solution)/shard_map/reduce_scatter | solution.py:242
  844.6 55.5 %reduce-scatter.76.cloned.1.call-start = ((), (), s32[]{:S(2)}) async-start(), calls=%async_computation.48 | async-start | bytes 786432 | tf_op jit(solution)/shard_map/reduce_scatter | solution.py:245
  851.0 53.4 %reduce-scatter.94.cloned.1.call-start = ((), (), s32[]{:S(2)}) async-start(), calls=%async_computation.60 | async-start | bytes 1310720 | tf_op jit(solution)/shard_map/reduce_scatter | solution.py:73
  877.2 54.7 %reduce-scatter.78.cloned.1.call-start = ((), (), s32[]{:S(2)}) async-start(), calls=%async_computation.49 | async-start | bytes 1310720 | tf_op jit(solution)/shard_map/reduce_scatter | solution.py:73
  937.3 63.0 %reduce-scatter.96.cloned.1.call-start = ((), (), s32[]{:S(2)}) async-start(), calls=%async_computation.62 | async-start | bytes 1310720 | tf_op jit(solution)/shard_map/reduce_scatter | solution.py:73
  962.0 66.4 %reduce-scatter.80.cloned.1.call-start = ((), (), s32[]{:S(2)}) async-start(), calls=%async_computation.51 | async-start | bytes 1310720 | tf_op jit(solution)/shard_map/reduce_scatter | solution.py:73
  980.0 70.5 %all-gather.57.cloned.1.call-start = ((), (), s32[]{:S(2)}) async-start(), calls=%async_computation.63 | async-start | bytes 1310720 | tf_op jit(solution)/shard_map/all_gather | solution.py:63
  1034.5 114.7 %reduce-scatter.98.cloned.1.call-start = ((), (), s32[]{:S(2)}) async-start(), calls=%async_computation.64 | async-start | bytes 786432 | tf_op jit(solution)/shard_map/reduce_scatter | solution.py:242
  1077.9 71.3 %reduce-scatter.100.cloned.1.call-start = ((), (), s32[]{:S(2)}) async-start(), calls=%async_computation.65 | async-start | bytes 786432 | tf_op jit(solution)/shard_map/reduce_scatter | solution.py:245
  1086.1 88.9 %reduce-scatter.82.cloned.1.call-start = ((), (), s32[]{:S(2)}) async-start(), calls=%async_computation.53 | async-start | bytes 786432 | tf_op jit(solution)/shard_map/reduce_scatter | solution.py:242
  1117.7 57.4 %reduce-scatter.84.cloned.1.call-start = ((), (), s32[]{:S(2)}) async-start(), calls=%async_computation.54 | async-start | bytes 786432 | tf_op jit(solution)/shard_map/reduce_scatter | solution.py:245
  1125.8 98.7 %reduce-scatter.102.cloned.1.call-start = ((), (), s32[]{:S(2)}) async-start(), calls=%async_computation.66 | async-start | bytes 1310720 | tf_op jit(solution)/shard_map/reduce_scatter | solution.py:73
  1152.9 71.7 %reduce-scatter.86.cloned.1.call-start = ((), (), s32[]{:S(2)}) async-start(), calls=%async_computation.55 | async-start | bytes 1310720 | tf_op jit(solution)/shard_map/reduce_scatter | solution.py:73
  1178.7 56.8 %reduce-scatter.106.cloned.1.call-start = ((), (), s32[]{:S(2)}) async-start(), calls=%async_computation.68 | async-start | bytes 1310720 | tf_op jit(solution)/shard_map/reduce_scatter | solution.py:357
  1184.1 129.2 %reduce-scatter.110.cloned.1.call-start = ((), (), s32[]{:S(2)}) async-start(), calls=%async_computation.70 | async-start | bytes 5242880 | tf_op jit(solution)/shard_map/reduce_scatter | solution.py:375
  1194.2 198.7 %reduce-scatter.108.cloned.1.call-start = ((), (), s32[]{:S(2)}) async-start(), calls=%async_computation.69 | async-start | bytes 5242880 | tf_op jit(solution)/shard_map/reduce_scatter | solution.py:369
  1205.4 250.8 %reduce-scatter.104.cloned.1.call-start = ((), (), s32[]{:S(2)}) async-start(), calls=%async_computation.67 | async-start | bytes 3932160 | tf_op jit(solution)/shard_map/reduce_scatter | solution.py:348
  1216.5 261.6 %reduce-scatter.128.cloned.1.call-start = ((), (), s32[]{:S(2)}) async-start(), calls=%async_computation.87 | async-start | bytes 327680
  1218.4 279.1 %reduce-scatter.126.cloned.1.call-start = ((), (), s32[]{:S(2)}) async-start(), calls=%async_computation.86 | async-start | bytes 20480
  1219.4 298.1 %reduce-scatter.124.cloned.1.call-start = ((), (), s32[]{:S(2)}) async-start(), calls=%async_computation.85 | async-start | bytes 327680
  1220.4 317.1 %reduce-scatter.122.cloned.1.call-start = ((), (), s32[]{:S(2)}) async-start(), calls=%async_computation.84 | async-start | bytes 327680
  1221.4 336.9 %reduce-scatter.120.cloned.1.call-start = ((), (), s32[]{:S(2)}) async-start(), calls=%async_computation.83 | async-start | bytes 327680
  1222.4 355.7 %reduce-scatter.116.cloned.1.call-start = ((), (), s32[]{:S(2)}) async-start(), calls=%async_computation.81 | async-start | bytes 20480
  1223.3 374.1 %reduce-scatter.118.cloned.1.call-start = ((), (), s32[]{:S(2)}) async-start(), calls=%async_computation.82 | async-start | bytes 20480
  1224.5 393.5 %reduce-scatter.114.cloned.1.call-start = ((), (), s32[]{:S(2)}) async-start(), calls=%async_computation.80 | async-start | bytes 327680
  1228.7 410.0 %reduce-scatter.112.cloned.1.call-start = ((), (), s32[]{:S(2)}) async-start(), calls=%async_computation.79 | async-start | bytes 327680
  1229.7 496.3 %all-reduce.5.cloned.1.call-start = ((), (), s32[]{:S(2)}) async-start(), calls=%async_computation.88 | async-start | bytes 6291456 | tf_op jit(solution)/shard_map/psum | solution.py:383
  (206 other events, 3570.1 us)
Sparse Core Ops, SparseCore 0:
  10.2 48.8 all-gather.58
  117.0 24.9 reduce-scatter.55
  188.6 26.4 reduce-scatter.63
  217.1 46.2 all-gather.60
  265.3 45.1 all-gather.62
  314.9 23.1 reduce-scatter.57
  340.8 24.8 reduce-scatter.65
  367.8 45.2 all-gather.64
  464.6 24.9 reduce-scatter.67
  492.8 24.8 reduce-scatter.59
  519.8 46.3 all-gather.66
  567.6 15.5 all-gather.72
  585.4 46.2 all-gather.68
  633.1 14.9 all-gather.70
  650.4 24.8 reduce-scatter.87
  677.9 24.8 reduce-scatter.71
  705.2 24.8 reduce-scatter.61
  732.7 24.8 reduce-scatter.69
  762.0 16.7 all-gather.52
  780.7 16.7 all-gather.46
  844.7 14.6 reduce-scatter.73
  862.2 14.5 reduce-scatter.75
  879.3 25.0 reduce-scatter.93
  906.9 24.9 reduce-scatter.77
  936.7 16.7 all-gather.54
  955.6 16.7 all-gather.48
  975.4 24.8 reduce-scatter.95
  1003.5 24.8 reduce-scatter.79
  1033.7 16.7 all-gather.56
  1052.6 16.7 all-gather.50
  1078.0 14.5 reduce-scatter.97
  1117.8 14.6 reduce-scatter.81
  1153.0 24.9 reduce-scatter.101
  1181.2 24.8 reduce-scatter.85
  1208.3 27.1 reduce-scatter.105
  1237.9 75.4 reduce-scatter.109
  1315.7 77.2 reduce-scatter.107
  1395.4 60.7 reduce-scatter.103
  1458.4 19.6 reduce-scatter.127
  1480.3 17.1 reduce-scatter.125
  1499.7 17.7 reduce-scatter.123
  1519.6 17.8 reduce-scatter.121
  1540.3 17.9 reduce-scatter.119
  1560.9 17.1 reduce-scatter.115
  1580.3 17.0 reduce-scatter.117
  1600.2 17.7 reduce-scatter.113
  1620.7 17.9 reduce-scatter.111
  1641.2 84.7 all-reduce.4
  (4 shorter events, 57.9 us)
